TPU v7x, 512 devices: a whole 4x4x16 slice. The times are simulated.
512 devices in a mesh: dp: 4 (over x), ctx: 32 (over z, core), tp: 4 (over y).
Axes of the slice: x: 4, y: 4, z: 16, core: 2. Of those that a mesh axis runs over, the one named last changes fastest.
Arguments:
- inputs: bfloat16 [4, 4096, 8192], P('dp', 'ctx', 'tp'), may hold values from -6 to 6
- grad_out: bfloat16 [4, 4096, 8192], P('dp', 'ctx', 'tp'), may hold values from -6 to 6
- input_map: bfloat16 [4, 4096, 128], P('dp', 'ctx'), may hold values from -0.5 to 0.5
- output_map: bfloat16 [4, 4096, 128], P('dp', 'ctx'), may hold values from -0.25 to 0.25
- step_size: float32 [4, 128, 4096], P('dp', 'tp', 'ctx'), may hold values from 0.3 to 1.5
- log_decay: float32 [4, 128, 4096], P('dp', 'tp', 'ctx'), may hold values from -2 to 0
- skip_gain: float32 [128], P('tp'), may hold values from 0.5 to 1.5
Outputs:
- mixed: bfloat16 [4, 4096, 8192], P('dp', 'ctx', 'tp')
- grad_inputs: bfloat16 [4, 4096, 8192], P('dp', 'ctx', 'tp')
- grad_step: float32 [4, 128, 4096], P('dp', 'tp', 'ctx')
- grad_decay: float32 [4, 128, 4096], P('dp', 'tp', 'ctx')
- grad_input_map: float32 [4, 4096, 128], P('dp', ('ctx', 'tp'))
- grad_output_map: float32 [4, 4096, 128], P('dp', ('ctx', 'tp'))
- grad_skip: float32 [128], P('tp')
All inputs are finite; a program needn't handle non-finite values.
Results may differ from a plain program's by a relative error of at most 0.0011.
Values sent between devices are 32-bit elements; how exact they have to be, the bound alone decides.
No kernel may reach another device: no remote copies, remote signals or barrier semaphores. Data moves between devices by JAX's collectives and lax.ppermute only.
A program may use at most 192 MiB of HBM per device.

v0:
```python
import math
import jax
import jax.numpy as jnp
from jax import lax
from jax.sharding import PartitionSpec as P

precise = lax.Precision.HIGHEST


def entering(part, axis, combine, identity, reverse):
    count = lax.axis_size(axis)
    place = lax.axis_index(axis)
    ahead = count - 1 - place if reverse else place
    gathered = jax.tree.map(lambda a: lax.all_gather(a, axis), part)
    state = jax.tree.map(lambda a, e: jnp.zeros_like(a) + jnp.asarray(e, a.dtype), part, identity)

    def one(hop, state):
        source = count - 1 - hop if reverse else hop
        return combine(
            state, jax.tree.map(lambda a: lax.dynamic_index_in_dim(a, source, 0, False), gathered)
        )

    return lax.fori_loop(0, ahead, one, state)


def combine_pair(earlier, later_part):
    return (earlier[0] * later_part[0], later_part[0][..., None, None] * earlier[1] + later_part[1])


def block_forward(values, in_map, out_map, steps, logs):
    cumulative = jnp.cumsum(logs, axis=-1)
    length = cumulative.shape[-1]
    row_ids = lax.broadcasted_iota(jnp.int32, (length, length), 0)
    column_ids = lax.broadcasted_iota(jnp.int32, (length, length), 1)
    causal = row_ids >= column_ids
    spread = cumulative[..., :, None] - cumulative[..., None, :]
    decays = jnp.where(causal, jnp.exp(jnp.where(causal, spread, 0.0)), 0.0)
    affinity = jnp.einsum("btn,bsn->bts", out_map, in_map, precision=precise)
    mixing = decays * affinity[:, None]
    scaled = values * jnp.transpose(steps, (0, 2, 1))[..., None]
    remain = jnp.exp(cumulative[..., -1:] - cumulative)
    weighted = remain[..., None] * in_map[:, None]
    local_state = jnp.einsum("bshp,bhsn->bhpn", scaled, weighted, precision=precise)
    through = jnp.exp(cumulative[..., -1])
    return (cumulative, decays, mixing, scaled, remain, local_state, through)


def block_output(values, out_map, skip_gain, cumulative, mixing, scaled, incoming):
    within = jnp.einsum("bhts,bshp->bthp", mixing, scaled, precision=precise)
    carried = jnp.einsum("bhpn,btn->bthp", incoming, out_map, precision=precise)
    carried = carried * jnp.transpose(jnp.exp(cumulative), (0, 2, 1))[..., None]
    return (within + carried + skip_gain[:, None] * values, carried)


def block_source(cotangent, out_map, cumulative):
    weighted = jnp.exp(cumulative)[..., None] * out_map[:, None]
    return jnp.einsum("bshp,bhsn->bhpn", cotangent, weighted, precision=precise)


def block_backward(
    values,
    cotangent,
    in_map,
    out_map,
    steps,
    skip_gain,
    cumulative,
    decays,
    mixing,
    scaled,
    remain,
    local_state,
    through,
    incoming,
    carried,
    arriving,
):
    remain_col = jnp.transpose(remain, (0, 2, 1))[..., None]
    starts = jnp.transpose(jnp.exp(cumulative), (0, 2, 1))[..., None]
    steps_col = jnp.transpose(steps, (0, 2, 1))[..., None]
    from_later = jnp.einsum("bhpn,btn->bthp", arriving, in_map, precision=precise)
    state_grad = (
        jnp.einsum("bhst,bshp->bthp", mixing, cotangent, precision=precise)
        + remain_col * from_later
    )
    grad_values = steps_col * state_grad + skip_gain[:, None] * cotangent
    grad_steps = jnp.transpose(jnp.sum(values * state_grad, axis=-1), (0, 2, 1))
    products = jnp.einsum("bthp,bshp->bhts", cotangent, scaled, precision=precise)
    summed = jnp.sum(decays * products, axis=1)
    grad_in_map = jnp.einsum("bts,btn->bsn", summed, out_map, precision=precise) + jnp.einsum(
        "bthp,bhpn->btn", scaled * remain_col, arriving, precision=precise
    )
    grad_out_map = jnp.einsum("bts,bsn->btn", summed, in_map, precision=precise) + jnp.einsum(
        "bthp,bhpn->btn", cotangent * starts, incoming, precision=precise
    )
    paired = mixing * products
    change = jnp.sum(paired, axis=-1) - jnp.sum(paired, axis=-2)
    change = change + jnp.transpose(jnp.sum(cotangent * carried, axis=-1), (0, 2, 1))
    change = change - remain * jnp.transpose(jnp.sum(scaled * from_later, axis=-1), (0, 2, 1))
    final_edge = jnp.sum(arriving * local_state, axis=(2, 3)) + through * jnp.sum(
        arriving * incoming, axis=(2, 3)
    )
    length = change.shape[-1]
    ending = lax.broadcasted_iota(jnp.int32, (length,), 0) == length - 1
    change = change + jnp.where(ending, final_edge[..., None], 0.0)
    grad_logs = lax.cumsum(change, axis=2, reverse=True)
    skip_part = jnp.sum(cotangent * values, axis=(0, 1, 3))
    return (grad_values, grad_steps, grad_in_map, grad_out_map, grad_logs, skip_part)


def shards(inputs, grad_out, input_map, output_map, step_size, log_decay, skip_gain):
    sequences, length, features = inputs.shape
    heads = step_size.shape[1]
    per_head = features // heads
    values = inputs.reshape(sequences, length, heads, per_head).astype(jnp.float32)
    cotangent = grad_out.reshape(sequences, length, heads, per_head).astype(jnp.float32)
    in_map = input_map.astype(jnp.float32)
    out_map = output_map.astype(jnp.float32)
    cumulative, decays, mixing, scaled, remain, local_state, through = block_forward(
        values, in_map, out_map, step_size, log_decay
    )
    source = block_source(cotangent, out_map, cumulative)
    neutral = (jnp.ones_like(through), jnp.zeros_like(local_state))
    ahead = entering((through, local_state), "ctx", combine_pair, neutral, False)
    behind = entering((through, source), "ctx", combine_pair, neutral, True)
    incoming = ahead[1]
    arriving = behind[1]
    mixed, carried = block_output(values, out_map, skip_gain, cumulative, mixing, scaled, incoming)
    results = block_backward(
        values,
        cotangent,
        in_map,
        out_map,
        step_size,
        skip_gain,
        cumulative,
        decays,
        mixing,
        scaled,
        remain,
        local_state,
        through,
        incoming,
        carried,
        arriving,
    )
    grad_values, grad_steps, grad_in_part, grad_out_part, grad_logs, skip_part = results
    grad_in_map, grad_out_map = (
        lax.psum_scatter(grad_in_part, "tp", scatter_dimension=1, tiled=True),
        lax.psum_scatter(grad_out_part, "tp", scatter_dimension=1, tiled=True),
    )
    skip_total = lax.psum(skip_part, ("dp", "ctx"))
    factor = 1.0 / math.sqrt(
        sequences * lax.axis_size("dp") * length * lax.axis_size("ctx") * per_head
    )
    mixed_out = mixed.reshape(sequences, length, features).astype(jnp.bfloat16)
    grad_inputs = grad_values.reshape(sequences, length, features).astype(jnp.bfloat16)
    return (
        mixed_out,
        grad_inputs,
        grad_steps,
        grad_logs,
        grad_in_map,
        grad_out_map,
        skip_total * factor,
    )


def solution(mesh):
    in_specs = (
        P("dp", "ctx", "tp"),
        P("dp", "ctx", "tp"),
        P("dp", "ctx", None),
        P("dp", "ctx", None),
        P("dp", "tp", "ctx"),
        P("dp", "tp", "ctx"),
        P("tp"),
    )
    out_specs = (
        P("dp", "ctx", "tp"),
        P("dp", "ctx", "tp"),
        P("dp", "tp", "ctx"),
        P("dp", "tp", "ctx"),
        P("dp", ("ctx", "tp"), None),
        P("dp", ("ctx", "tp"), None),
        P("tp"),
    )
    return jax.shard_map(shards, mesh=mesh, in_specs=in_specs, out_specs=out_specs, check_vma=False)
```

profile of v0, /device:TPU:2, one launch (start us, length us, event | category | flops | bytes accessed | tf_op | source)
XLA Modules:
  0.0 737.4 jit_solution(14283848565593800011)
XLA Ops:
  9.9 3.2 fusion.3
  13.5 2.4 fusion.16
  16.1 36.1 %all-gather = f32[32,32,1]{1,2,0:T(1,128)S(1)} all-gather(f32[1,32,1]{1,2,0:T(1,128)S(1)} %exp.61), channel_id=2, replica_groups=mesh['dp'=4,'ctx'=32,'tp'=4] {'ctx'}, dimensions={0}, use_global_device_ids=true | all-gather | bytes 4224 | tf_op jit(solution)/shard_map/all_gather | solution.py:14
  52.3 3.1 fusion.20
  55.4 153.7 %all-gather.6.cloned.1.call-done = f32[1024,64,128]{2,1,0:T(8,128)} async-done(((f32[32,64,128]{2,1,0:T(8,128)}), f32[1024,64,128]{2,1,0:T(8,128)}) %all-gather.6.cloned.1.call-update) | async-done | bytes 33554448 | tf_op jit(solution)/shard_map/all_gather | solution.py:14
  209.2 191.1 %all-gather.8.cloned.1.call-done = f32[1024,64,128]{2,1,0:T(8,128)} async-done(((f32[32,64,128]{2,1,0:T(8,128)}), f32[1024,64,128]{2,1,0:T(8,128)}) %all-gather.8.cloned.1.call-update) | async-done | bytes 33554448 | tf_op jit(solution)/shard_map/all_gather | solution.py:14
  400.4 46.3 %while.27 = (s32[]{:T(128)}, f32[1,32,64,128]{3,2,1,0:T(8,128)S(1)}, s32[]{:T(128)}, f32[32,1,32]{2,1,0:T(1,128)S(1)}, f32[32,1,32,64,128]{4,3,2,1,0:T(8,128)}, ...) while((s32[]{:T(128)}, f32[1,32,64,128]{3,2,1,0:T(8,128)S(1)}, s32[]{:T(128)}, f32[32,1,32]{2,1,0:T(1,128)S(1)}, ...), condition=%wide.region_4.5_spmd, body=%wide.region_3.4_spmd.sunk | while | flops 524294 | bytes 3146259 | solution.py:23
  400.4 1.4 bitcast_add_fusion.6
  401.9 1.4 bitcast_add_fusion.6
  403.4 1.4 bitcast_add_fusion.6
  404.9 1.4 bitcast_add_fusion.6
  406.4 1.4 bitcast_add_fusion.6
  407.9 1.4 bitcast_add_fusion.6
  409.4 1.4 bitcast_add_fusion.6
  410.9 1.4 bitcast_add_fusion.6
  412.4 1.4 bitcast_add_fusion.6
  413.9 1.4 bitcast_add_fusion.6
  415.4 1.4 bitcast_add_fusion.6
  416.9 1.4 bitcast_add_fusion.6
  418.3 1.4 bitcast_add_fusion.6
  419.8 1.4 bitcast_add_fusion.6
  434.8 1.4 bitcast_add_fusion.6
  443.8 1.4 bitcast_add_fusion.6
  446.7 1.6 multiply_reduce_fusion.2
  449.4 1.6 multiply_reduce_fusion.3
  452.4 1.9 convolution_bitcast_fusion.2
  455.5 3.8 fusion.31
  459.3 3.2 multiply_reduce_fusion.4
  462.4 1.9 convolution_bitcast_fusion.3
  466.5 208.1 %psum.7 = f32[32]{0:T(128)S(1)} all-reduce(f32[32]{0:T(128)S(1)} %reduce_sum.113), channel_id=1, replica_groups=mesh['dp'=4,'ctx'=32,'tp'=4] {'dp','ctx'}, use_global_device_ids=true, to_apply=%region_18.19 | all-reduce | flops 32 | bytes 256 | tf_op jit(solution)/shard_map/psum | solution.py:152
  675.4 1.8 reduce_window_sum.22
  677.8 53.1 %reduce-scatter.3.cloned.1.call-done = f32[1,32,128]{2,1,0:T(8,128)} async-done(((f32[1,128,128]{2,1,0:T(8,128)}), f32[1,32,128]{2,1,0:T(8,128)}) %reduce-scatter.3.cloned.1.call-update) | async-done | bytes 16400 | tf_op jit(solution)/shard_map/reduce_scatter | solution.py:149
  (109 shorter events, 32.5 us)
Async XLA Ops:
  7.2 2.7 copy-start.8
  7.2 2.8 copy-start.11
  7.2 201.8 %all-gather.6.cloned.1.call-start = ((), (), s32[]{:S(2)}) async-start(), calls=%async_computation.4 | async-start | bytes 34603008 | tf_op jit(solution)/shard_map/all_gather | solution.py:14
  9.8 3.3 copy-start.4
  9.8 3.4 copy-start.10
  9.9 3.6 copy-start.9
  13.1 387.1 %all-gather.8.cloned.1.call-start = ((), (), s32[]{:S(2)}) async-start(), calls=%async_computation.5 | async-start | bytes 34603008 | tf_op jit(solution)/shard_map/all_gather | solution.py:14
  13.5 41.9 %copy-start.1 = (bf16[1,128,2048]{1,2,0:T(8,128)(2,1)}, bf16[1,128,2048]{1,2,0:T(8,128)(2,1)S(1)}, u32[]{:S(2)}) copy-start(bf16[1,128,2048]{1,2,0:T(8,128)(2,1)S(1)} %copy.84) | copy-start | bytes 1572868
  16.0 661.8 %reduce-scatter.5.cloned.1.call-start = ((), (), s32[]{:S(2)}) async-start(), calls=%async_computation.3 | async-start | bytes 81920 | tf_op jit(solution)/shard_map/reduce_scatter | solution.py:150
  446.7 1.6 copy-start
  448.3 1.0 copy-start.2
  449.4 1.7 copy-start.5
  451.1 4.3 copy-start.12
  455.2 275.7 %reduce-scatter.3.cloned.1.call-start = ((), (), s32[]{:S(2)}) async-start(), calls=%async_computation.2 | async-start | bytes 81920 | tf_op jit(solution)/shard_map/reduce_scatter | solution.py:149
  455.4 3.8 copy-start.3
  455.5 3.8 copy-start.7
  459.3 3.2 copy-start.6
Sparse Core Ops, SparseCore 0:
  13.3 195.7 all-gather.5
  211.1 189.0 all-gather.7
  455.3 18.9 reduce-scatter.4
  675.5 55.2 reduce-scatter.2
where the time goes:
time: 739 us; the launch traced here: 737 us
  waiting for transfers between devices  398 us (54%)
  blocking collectives  244 us (33%)
  other arithmetic  50.2 us (7%)
  matrix products  24.4 us (3%)
  between operations  14.1 us (2%)
    all_gather x2, waiting for transfers between devices, entering(): gathered = jax.tree.map(lambda a: lax.all_gather(a, axis), part)  345 us
    psum x1, blocking collectives, shards(): skip_total = lax.psum(skip_part, ('dp', 'ctx'))  208 us
    reduce_scatter x1, waiting for transfers between devices, shards(): lax.psum_scatter(grad_in_part, 'tp', scatter_dimension=1, tiled=True)  53.1 us
    add x31, other arithmetic, combine_pair(): later_part[0][..., None, None] * earlier[1] + later_part[1]  44.9 us
    all_gather x1, blocking collectives, entering(): gathered = jax.tree.map(lambda a: lax.all_gather(a, axis), part)  36.1 us
  transfers between devices with their start and end apart: 4, of which 3 were waited for; matrix products, arithmetic and copies ran while one was open for 3% of the time, Pallas kernels for 0%

commit v1 on v0

--- a/solution.py
+++ b/solution.py
@@ -149,7 +149,7 @@
         lax.psum_scatter(grad_in_part, "tp", scatter_dimension=1, tiled=True),
         lax.psum_scatter(grad_out_part, "tp", scatter_dimension=1, tiled=True),
     )
-    skip_total = lax.psum(skip_part, ("dp", "ctx"))
+    skip_total = lax.psum(lax.psum(skip_part, "dp"), "ctx")
     factor = 1.0 / math.sqrt(
         sequences * lax.axis_size("dp") * length * lax.axis_size("ctx") * per_head
     )

time: 739 us -> 549 us (0.74)
  blocking collectives: 244 us -> 90.4 us
  waiting for transfers between devices: 398 us -> 361 us
    psum x1 -> x2, blocking collectives: 208 us -> 54.4 us  [shards(): skip_total = lax.psum(lax.psum(skip_part, 'dp'), 'ctx')]
    reduce_scatter x1, waiting for transfers between devices: 53.1 us -> 16.5 us  [shards(): lax.psum_scatter(grad_in_part, 'tp', scatter_dimension=1, tiled=True)]
  transfers between devices with their start and end apart: 4 -> 4, of which waited for: 3 -> 3; matrix products, arithmetic and copies ran while one was open for 3% -> 4% of each run, Pallas kernels for 0% -> 0%
where the time goes in v1:
time: 549 us; the launch traced here: 547 us
  waiting for transfers between devices  361 us (66%)
  blocking collectives  90.4 us (16%)
  other arithmetic  50.2 us (9%)
  matrix products  24.4 us (4%)
  between operations  14.1 us (3%)
    all_gather x2, waiting for transfers between devices, entering(): gathered = jax.tree.map(lambda a: lax.all_gather(a, axis), part)  345 us
    psum x2, blocking collectives, shards(): skip_total = lax.psum(lax.psum(skip_part, 'dp'), 'ctx')  54.4 us
    add x31, other arithmetic, combine_pair(): later_part[0][..., None, None] * earlier[1] + later_part[1]  44.9 us
    all_gather x1, blocking collectives, entering(): gathered = jax.tree.map(lambda a: lax.all_gather(a, axis), part)  36.1 us
    reduce_scatter x1, waiting for transfers between devices, shards(): lax.psum_scatter(grad_in_part, 'tp', scatter_dimension=1, tiled=True)  16.5 us
  transfers between devices with their start and end apart: 4, of which 3 were waited for; matrix products, arithmetic and copies ran while one was open for 4% of the time, Pallas kernels for 0%

profile of v1, /device:TPU:2, one launch (start us, length us, event | category | flops | bytes accessed | tf_op | source)
XLA Modules:
  0.0 547.1 jit_solution(5717141025166187131)
XLA Ops:
  9.9 3.2 fusion.3
  13.5 2.4 fusion.16
  16.1 36.1 %all-gather = f32[32,32,1]{1,2,0:T(1,128)S(1)} all-gather(f32[1,32,1]{1,2,0:T(1,128)S(1)} %exp.61), channel_id=2, replica_groups=mesh['dp'=4,'ctx'=32,'tp'=4] {'ctx'}, dimensions={0}, use_global_device_ids=true | all-gather | bytes 4224 | tf_op jit(solution)/shard_map/all_gather | solution.py:14
  52.3 3.1 fusion.20
  55.4 153.7 %all-gather.6.cloned.1.call-done = f32[1024,64,128]{2,1,0:T(8,128)} async-done(((f32[32,64,128]{2,1,0:T(8,128)}), f32[1024,64,128]{2,1,0:T(8,128)}) %all-gather.6.cloned.1.call-update) | async-done | bytes 33554448 | tf_op jit(solution)/shard_map/all_gather | solution.py:14
  209.2 191.1 %all-gather.8.cloned.1.call-done = f32[1024,64,128]{2,1,0:T(8,128)} async-done(((f32[32,64,128]{2,1,0:T(8,128)}), f32[1024,64,128]{2,1,0:T(8,128)}) %all-gather.8.cloned.1.call-update) | async-done | bytes 33554448 | tf_op jit(solution)/shard_map/all_gather | solution.py:14
  400.4 46.3 %while.27 = (s32[]{:T(128)}, f32[1,32,64,128]{3,2,1,0:T(8,128)S(1)}, s32[]{:T(128)}, f32[32,1,32]{2,1,0:T(1,128)S(1)}, f32[32,1,32,64,128]{4,3,2,1,0:T(8,128)}, ...) while((s32[]{:T(128)}, f32[1,32,64,128]{3,2,1,0:T(8,128)S(1)}, s32[]{:T(128)}, f32[32,1,32]{2,1,0:T(1,128)S(1)}, ...), condition=%wide.region_4.5_spmd, body=%wide.region_3.4_spmd.sunk | while | flops 524294 | bytes 3146259 | solution.py:23
  400.4 1.4 bitcast_add_fusion.6
  401.9 1.4 bitcast_add_fusion.6
  403.4 1.4 bitcast_add_fusion.6
  404.9 1.4 bitcast_add_fusion.6
  406.4 1.4 bitcast_add_fusion.6
  407.9 1.4 bitcast_add_fusion.6
  409.4 1.4 bitcast_add_fusion.6
  410.9 1.4 bitcast_add_fusion.6
  412.4 1.4 bitcast_add_fusion.6
  413.9 1.4 bitcast_add_fusion.6
  415.4 1.4 bitcast_add_fusion.6
  416.9 1.4 bitcast_add_fusion.6
  418.3 1.4 bitcast_add_fusion.6
  434.8 1.4 bitcast_add_fusion.6
  443.8 1.4 bitcast_add_fusion.6
  446.7 1.6 multiply_reduce_fusion.2
  449.4 1.6 multiply_reduce_fusion.3
  452.4 1.9 convolution_bitcast_fusion.2
  455.5 3.8 fusion.31
  459.3 3.2 multiply_reduce_fusion.4
  462.4 1.9 convolution_bitcast_fusion.3
  466.5 8.6 %psum.14 = f32[32]{0:T(128)S(1)} all-reduce(f32[32]{0:T(128)S(1)} %reduce_sum.113), channel_id=1, replica_groups=mesh['dp'=4,'ctx'=32,'tp'=4] {'dp'}, use_global_device_ids=true, to_apply=%region_18.19 | all-reduce | flops 32 | bytes 256 | tf_op jit(solution)/shard_map/psum | solution.py:152
  475.1 45.8 %psum.15 = f32[32]{0:T(128)S(1)} all-reduce(f32[32]{0:T(128)S(1)} %psum.14), channel_id=1, replica_groups=mesh['dp'=4,'ctx'=32,'tp'=4] {'ctx'}, use_global_device_ids=true, to_apply=%region_19.20 | all-reduce | flops 32 | bytes 256 | tf_op jit(solution)/shard_map/psum | solution.py:152
  521.7 1.8 reduce_window_sum.22
  524.1 16.5 %reduce-scatter.3.cloned.1.call-done = f32[1,32,128]{2,1,0:T(8,128)} async-done(((f32[1,128,128]{2,1,0:T(8,128)}), f32[1,32,128]{2,1,0:T(8,128)}) %reduce-scatter.3.cloned.1.call-update) | async-done | bytes 16400 | tf_op jit(solution)/shard_map/reduce_scatter | solution.py:149
  (110 shorter events, 33.9 us)
Async XLA Ops:
  7.2 2.7 copy-start.8
  7.2 2.8 copy-start.11
  7.2 201.8 %all-gather.6.cloned.1.call-start = ((), (), s32[]{:S(2)}) async-start(), calls=%async_computation.4 | async-start | bytes 34603008 | tf_op jit(solution)/shard_map/all_gather | solution.py:14
  9.8 3.3 copy-start.4
  9.8 3.4 copy-start.10
  9.9 3.6 copy-start.9
  13.1 387.1 %all-gather.8.cloned.1.call-start = ((), (), s32[]{:S(2)}) async-start(), calls=%async_computation.5 | async-start | bytes 34603008 | tf_op jit(solution)/shard_map/all_gather | solution.py:14
  13.5 41.9 %copy-start.1 = (bf16[1,128,2048]{1,2,0:T(8,128)(2,1)}, bf16[1,128,2048]{1,2,0:T(8,128)(2,1)S(1)}, u32[]{:S(2)}) copy-start(bf16[1,128,2048]{1,2,0:T(8,128)(2,1)S(1)} %copy.84) | copy-start | bytes 1572868
  16.0 508.1 %reduce-scatter.5.cloned.1.call-start = ((), (), s32[]{:S(2)}) async-start(), calls=%async_computation.3 | async-start | bytes 81920 | tf_op jit(solution)/shard_map/reduce_scatter | solution.py:150
  446.7 1.6 copy-start
  448.3 1.0 copy-start.2
  449.4 1.7 copy-start.5
  451.1 4.3 copy-start.12
  455.2 85.4 %reduce-scatter.3.cloned.1.call-start = ((), (), s32[]{:S(2)}) async-start(), calls=%async_computation.2 | async-start | bytes 81920 | tf_op jit(solution)/shard_map/reduce_scatter | solution.py:149
  455.4 3.8 copy-start.3
  455.5 3.8 copy-start.7
  459.3 3.2 copy-start.6
Sparse Core Ops, SparseCore 0:
  13.3 195.7 all-gather.5
  211.1 189.0 all-gather.7
  455.3 18.9 reduce-scatter.4
  521.8 18.6 reduce-scatter.2
